TPU v7x, 512 devices: a whole 4x4x16 slice. The times are simulated.
512 devices in a mesh: rowpt: 32 (over y, z_hi, core), colpt: 16 (over z_lo, x).
Axes of the slice: x: 4, y: 4, z: 16 (z_hi: 4, z_lo: 4; z = z_hi * 4 + z_lo), core: 2. Of those that a mesh axis runs over, the one named last changes fastest.
Arguments:
- x_pairs: float32 [4, 1024, 1024], P(None, 'rowpt', 'colpt'), may hold values from -6 to 6
- eps_val: float32 [1024], P('rowpt'), may hold values from -2 to -0.5
- eps_con: float32 [1024], P('colpt'), may hold values from 0.5 to 2
- orb_val: float32 [8192, 1024], P(('rowpt', 'colpt')), may hold values from -0.35 to 0.35
- orb_con: float32 [8192, 1024], P(('rowpt', 'colpt')), may hold values from -0.35 to 0.35
- screened_w: float32 [8192, 8192], P('rowpt', 'colpt'), may hold values from -0.0625 to 0.0625
Outputs:
- hx: float32 [4, 1024, 1024], P(None, 'rowpt', 'colpt')
All inputs are finite; a program needn't handle non-finite values.
Results may differ from a plain program's by a relative error of at most 0.00005.
Values sent between devices are 32-bit elements; how exact they have to be, the bound alone decides.
A program may use at most 64 MiB of HBM per device.

v0:
```python
import jax
import jax.numpy as jnp
from jax import lax
from jax.sharding import PartitionSpec as P

NP = 8192


def joined_along(pieces, dim):
    lengths = list(pieces.shape[1:])
    lengths[dim] *= pieces.shape[0]
    return jnp.moveaxis(pieces, 0, dim).reshape(lengths)


def copy_for_each(array, axis):
    copies = jnp.broadcast_to(array, (lax.axis_size(axis), *array.shape))
    return lax.all_to_all(copies, axis, split_axis=0, concat_axis=0, tiled=True)


def gathered_copies(array, axis, dim):
    return joined_along(copy_for_each(array, axis), dim)


def in_blocks(array, dim, devices):
    lengths = array.shape
    pieces = array.reshape(*lengths[:dim], devices, lengths[dim] // devices, *lengths[dim + 1 :])
    return jnp.moveaxis(pieces, dim, 0)


def sent_and_summed(array, axis, dim):
    devices = lax.axis_size(axis)
    pieces = lax.all_to_all(in_blocks(array, dim, devices), axis, 0, 0, tiled=True)
    return jnp.sum(pieces, axis=0)


def over_copies(array, axis):
    everything = copy_for_each(array, axis)
    return jnp.sum(everything, axis=0)


def reorder_points(values, outer, inner):
    width = values.shape[1]
    shaped = values.reshape(outer, inner, -1, width)
    return jnp.transpose(shaped, (1, 0, 2, 3)).reshape(-1, width)


def per_device(x_pairs, eps_val, eps_con, orb_val, orb_con, screened_w):
    nrow = lax.axis_size("rowpt")
    ncol = lax.axis_size("colpt")
    val_part = lax.all_to_all(orb_val, "rowpt", split_axis=1, concat_axis=0, tiled=True)
    val_mixed = gathered_copies(val_part, "colpt", 0)
    val_cols = reorder_points(val_mixed, ncol, nrow)
    con_part = lax.all_to_all(orb_con, "colpt", split_axis=1, concat_axis=0, tiled=True)
    con_cols = lax.all_gather(con_part, "rowpt", axis=0, tiled=True)
    block_pts = min(NP, 2048)
    nblocks = NP // block_pts
    vecs = x_pairs.shape[0]
    val_blocks = val_cols.reshape(nblocks, block_pts, val_cols.shape[1])
    con_blocks = con_cols.reshape(nblocks, block_pts, con_cols.shape[1])

    def density_block(pieces):
        val_piece, con_piece = pieces
        through = jnp.einsum("pc,bvc->bpv", con_piece, x_pairs, precision=lax.Precision.HIGHEST)
        return jnp.sum(through * val_piece[None], axis=2)

    partial_density = lax.map(density_block, (val_blocks, con_blocks))
    partial_density = jnp.transpose(partial_density, (1, 0, 2)).reshape(vecs, NP)
    column_share = sent_and_summed(partial_density, "colpt", 1)
    density = over_copies(column_share, "rowpt")
    screened_part = jnp.einsum("bq,pq->bp", density, screened_w, precision=lax.Precision.HIGHEST)
    row_total = over_copies(screened_part, "colpt")
    screened = gathered_copies(row_total, "rowpt", 1)
    pot_blocks = jnp.transpose(screened.reshape(vecs, nblocks, block_pts), (1, 0, 2))

    def kernel_block(total, pieces):
        val_piece, con_piece, pot_piece = pieces
        weighted = val_piece[None] * pot_piece[:, :, None]
        step = jnp.einsum("bpv,pc->bvc", weighted, con_piece, precision=lax.Precision.HIGHEST)
        return (total + step, None)

    start = jnp.zeros(x_pairs.shape, jnp.float32)
    kernel, unused = lax.scan(kernel_block, start, (val_blocks, con_blocks, pot_blocks))
    diff = eps_con[None, None, :] - eps_val[None, :, None]
    return diff * x_pairs + kernel


def solution(mesh):
    in_specs = (
        P(None, "rowpt", "colpt"),
        P("rowpt"),
        P("colpt"),
        P(("rowpt", "colpt"), None),
        P(("rowpt", "colpt"), None),
        P("rowpt", "colpt"),
    )
    out_specs = P(None, "rowpt", "colpt")
    return jax.shard_map(
        per_device, mesh=mesh, in_specs=in_specs, out_specs=out_specs, check_vma=False
    )
```

profile of v0, /device:TPU:33, one launch (start us, length us, event | category | flops | bytes accessed | tf_op | source)
XLA Modules:
  0.0 252.5 jit_solution(8417644518098035840)
XLA Ops:
  6.5 1.0 all_to_all.48
  8.3 7.9 %all-to-all-start.2 = ((f32[16,1,1024]{2,1,0:T(1,128)}), f32[16,1,1024]{2,1,0:T(1,128)S(1)}, u32[]{:S(2)}, u32[]{:S(2)}) async-start(f32[16,1,1024]{2,1,0:T(1,128)} %reshape.48), calls=%async_computation.2 | async-start | bytes 131072 | tf_op jit(solution)/shard_map/all_to_all | solution.py:53
  18.2 3.8 %all-to-all-done.2 = f32[16,1,1024]{2,1,0:T(1,128)S(1)} async-done(((f32[16,1,1024]{2,1,0:T(1,128)}), f32[16,1,1024]{2,1,0:T(1,128)S(1)}, u32[]{:S(2)}, u32[]{:S(2)}) %all-to-all-start.2) | async-done | bytes 65568 | tf_op jit(solution)/shard_map/all_to_all | solution.py:53
  22.0 17.3 %all-to-all-start = ((f32[32,1,512]{2,1,0:T(1,128)}), f32[32,1,512]{2,1,0:T(1,128)S(1)}, u32[]{:S(2)}, u32[]{:S(2)}) async-start(f32[32,1,512]{2,1,0:T(1,128)} %reshape.46), calls=%async_computation | async-start | bytes 131072 | tf_op jit(solution)/shard_map/all_to_all | solution.py:50
  41.4 14.1 %all-to-all-done = f32[32,1,512]{2,1,0:T(1,128)S(1)} async-done(((f32[32,1,512]{2,1,0:T(1,128)}), f32[32,1,512]{2,1,0:T(1,128)S(1)}, u32[]{:S(2)}, u32[]{:S(2)}) %all-to-all-start) | async-done | bytes 65568 | tf_op jit(solution)/shard_map/all_to_all | solution.py:50
  56.6 1.1 broadcast_in_dim.28
  57.7 3.6 %all-to-all-start.1 = ((f32[16,512,32]{1,2,0:T(8,128)}), f32[16,512,32]{1,2,0:T(8,128)S(1)}, u32[]{:S(2)}, u32[]{:S(2)}) async-start(f32[16,512,32]{1,2,0:T(8,128)} %broadcast_in_dim.28), calls=%async_computation.1 | async-start | bytes 2097152 | tf_op jit(solution)/shard_map/all_to_all | solution.py:17
  61.3 33.9 %all-to-all-done.1 = f32[16,512,32]{1,2,0:T(8,128)S(1)} async-done(((f32[16,512,32]{1,2,0:T(8,128)}), f32[16,512,32]{1,2,0:T(8,128)S(1)}, u32[]{:S(2)}, u32[]{:S(2)}) %all-to-all-start.1) | async-done | bytes 1048608 | tf_op jit(solution)/shard_map/all_to_all | solution.py:17
  95.1 2.7 %copy.50 = f32[16,512,32]{2,1,0:T(8,128)} copy(f32[16,512,32]{1,2,0:T(8,128)S(1)} %all-to-all-done.1) | data formatting | bytes 2097152 | tf_op jit(solution)/shard_map/all_to_all | solution.py:17
  97.8 4.7 %copy.51 = f32[32,16,16,32]{3,2,1,0:T(8,128)} copy(f32[32,16,16,32]{3,2,0,1:T(8,128)} %bitcast.61) | data formatting | bytes 2097152 | tf_op jit(solution)/shard_map/transpose | solution.py:44
  102.5 3.7 %copy.60 = f32[4,2048,32]{1,2,0:T(8,128)} copy(f32[4,2048,32]{2,1,0:T(8,128)} %bitcast.62) | data formatting | bytes 2097152
  106.2 37.6 %all-gather.2.cloned.1.call-done = f32[8192,64]{1,0:T(8,128)} async-done(((f32[256,64]{1,0:T(8,128)}), f32[8192,64]{1,0:T(8,128)}) %all-gather.2.cloned.1.call-update) | async-done | bytes 2097168 | tf_op jit(solution)/shard_map/all_gather | solution.py:54
  143.8 2.9 %copy.54 = f32[4,2048,64]{1,2,0:T(8,128)S(1)} copy(f32[4,2048,64]{2,1,0:T(8,128)} %bitcast.63) | data formatting | bytes 4194304 | tf_op jit(solution)/shard_map/while | solution.py:66
  146.6 8.2 %while.21 = (s32[]{:T(128)}, f32[4,4,2048]{2,1,0:T(4,128)S(1)}, f32[4,2048,64]{1,2,0:T(8,128)S(1)}, f32[4,32,64]{2,1,0:T(8,128)S(1)}, f32[4,2048,32]{1,2,0:T(8,128)}, /*index=5*/s32[]{:T(128)}) while((s32[]{:T(128)}, f32[4,4,2048]{2,1,0:T(4,128)S(1)}, f32[4,2048,64]{1,2,0:T(8,128)S(1)}, f32[4,32,64]{2,1,0:T(8,128)S(1)}, ...), condition=%wide.region_2.3_spmd, body=%wide.region_0.2_spmd.sunk | while | flops 201842688 | bytes 1474641 | solution.py:66
  146.7 1.0 dynamic-slice_bitcast_fusion.6
  147.6 1.0 fusion.21
  148.7 1.0 dynamic-slice_bitcast_fusion.6
  149.7 1.0 fusion.21
  150.8 1.0 dynamic-slice_bitcast_fusion.6
  151.7 1.0 fusion.21
  152.8 1.0 dynamic-slice_bitcast_fusion.6
  153.8 1.0 fusion.21
  155.2 14.8 %all_to_all.63 = f32[16,4,512]{2,1,0:T(4,128)S(1)} all-to-all(f32[16,4,512]{2,1,0:T(4,128)S(1)} %copy.57), channel_id=1, replica_groups=mesh['rowpt'=32,'colpt'=16] {'colpt'}, dimensions={0} | all-to-all | bytes 262144 | tf_op jit(solution)/shard_map/all_to_all | solution.py:32
  170.0 32.2 %all_to_all.64 = f32[32,4,512]{2,1,0:T(4,128)S(1)} all-to-all(f32[32,4,512]{2,1,0:T(4,128)S(1)} %broadcast_in_dim.30), channel_id=1, replica_groups=mesh['rowpt'=32,'colpt'=16] {'rowpt'}, dimensions={0} | all-to-all | bytes 524288 | tf_op jit(solution)/shard_map/all_to_all | solution.py:17
  202.8 9.1 %all_to_all.65 = f32[16,4,256]{2,1,0:T(4,128)S(1)} all-to-all(f32[16,4,256]{2,1,0:T(4,128)S(1)} %broadcast_in_dim.31), channel_id=1, replica_groups=mesh['rowpt'=32,'colpt'=16] {'colpt'}, dimensions={0} | all-to-all | bytes 131072 | tf_op jit(solution)/shard_map/all_to_all | solution.py:17
  212.6 5.3 %all-to-all-start.6 = ((f32[32,4,256]{2,1,0:T(4,128)}), f32[32,4,256]{2,1,0:T(4,128)S(1)}, u32[]{:S(2)}, u32[]{:S(2)}) async-start(f32[32,4,256]{2,1,0:T(4,128)} %broadcast_in_dim.32), calls=%async_computation.6 | async-start | bytes 262144 | tf_op jit(solution)/shard_map/all_to_all | solution.py:17
  218.0 19.0 %all-to-all-done.6 = f32[32,4,256]{2,1,0:T(4,128)S(1)} async-done(((f32[32,4,256]{2,1,0:T(4,128)}), f32[32,4,256]{2,1,0:T(4,128)S(1)}, u32[]{:S(2)}, u32[]{:S(2)}) %all-to-all-start.6) | async-done | bytes 131104 | tf_op jit(solution)/shard_map/all_to_all | solution.py:17
  236.9 8.0 %while.22 = (s32[]{:T(128)}, f32[4,32,64]{2,1,0:T(8,128)S(1)}, f32[4,2048,32]{1,2,0:T(8,128)}, f32[4,4,2048]{2,1,0:T(4,128)S(1)}, f32[4,2048,64]{1,2,0:T(8,128)S(1)}, /*index=5*/s32[]{:T(128)}, s32[]{:T(128)}) while((s32[]{:T(128)}, f32[4,32,64]{2,1,0:T(8,128)S(1)}, f32[4,2048,32]{1,2,0:T(8,128)}, f32[4,4,2048]{2,1,0:T(4,128)S(1)}, ...), condition=%wide.region_7.8_spmd.clone, body=%wide.region_6.7_spmd.clone.sunk | while | flops 201605120 | bytes 1507427 | solution.py:82
  237.9 1.0 convolution_add_fusion.2
  239.9 1.0 convolution_add_fusion.2
  241.9 1.0 convolution_add_fusion.2
  244.0 1.0 convolution_add_fusion.2
  (47 shorter events, 12.2 us)
Async XLA Ops:
  6.5 195.7 %copy-start = (f32[256,512]{1,0:T(8,128)S(1)}, f32[256,512]{1,0:T(8,128)}, u32[]{:S(2)}) copy-start(f32[256,512]{1,0:T(8,128)} %param.15) | copy-start | bytes 1572868
  8.3 13.7 %all-to-all-start.2 = ((f32[16,1,1024]{2,1,0:T(1,128)}), f32[16,1,1024]{2,1,0:T(1,128)S(1)}, u32[]{:S(2)}, u32[]{:S(2)}) async-start(f32[16,1,1024]{2,1,0:T(1,128)} %reshape.48), calls=%async_computation.2 | async-start | bytes 131072 | tf_op jit(solution)/shard_map/all_to_all | solution.py:53
  22.0 33.5 %all-to-all-start = ((f32[32,1,512]{2,1,0:T(1,128)}), f32[32,1,512]{2,1,0:T(1,128)S(1)}, u32[]{:S(2)}, u32[]{:S(2)}) async-start(f32[32,1,512]{2,1,0:T(1,128)} %reshape.46), calls=%async_computation | async-start | bytes 131072 | tf_op jit(solution)/shard_map/all_to_all | solution.py:50
  39.3 104.5 %all-gather.2.cloned.1.call-start = ((), (), s32[]{:S(2)}) async-start(), calls=%async_computation.7 | async-start | bytes 4325376 | tf_op jit(solution)/shard_map/all_gather | solution.py:54
  57.7 37.4 %all-to-all-start.1 = ((f32[16,512,32]{1,2,0:T(8,128)}), f32[16,512,32]{1,2,0:T(8,128)S(1)}, u32[]{:S(2)}, u32[]{:S(2)}) async-start(f32[16,512,32]{1,2,0:T(8,128)} %broadcast_in_dim.28), calls=%async_computation.1 | async-start | bytes 2097152 | tf_op jit(solution)/shard_map/all_to_all | solution.py:17
  143.8 2.9 %copy-start.1 = (f32[4,32,64]{2,1,0:T(8,128)S(1)}, f32[4,32,64]{2,1,0:T(8,128)}, u32[]{:S(2)}) copy-start(f32[4,32,64]{2,1,0:T(8,128)} %param.10) | copy-start | bytes 98308
  154.9 63.0 %copy-start.2 = (f32[32]{0:T(128)S(1)}, f32[32]{0:T(128)}, u32[]{:S(2)}) copy-start(f32[32]{0:T(128)} %param.11) | copy-start | bytes 388
  154.9 63.0 %copy-start.3 = (f32[64]{0:T(128)S(1)}, f32[64]{0:T(128)}, u32[]{:S(2)}) copy-start(f32[64]{0:T(128)} %param.12) | copy-start | bytes 772
  212.6 24.3 %all-to-all-start.6 = ((f32[32,4,256]{2,1,0:T(4,128)}), f32[32,4,256]{2,1,0:T(4,128)S(1)}, u32[]{:S(2)}, u32[]{:S(2)}) async-start(f32[32,4,256]{2,1,0:T(4,128)} %broadcast_in_dim.32), calls=%async_computation.6 | async-start | bytes 262144 | tf_op jit(solution)/shard_map/all_to_all | solution.py:17
Sparse Core Ops, SparseCore 0:
  43.2 100.4 all-gather.1
where the time goes:
time: 253 us; the launch traced here: 252 us
  waiting for transfers between devices  108 us (43%)
  blocking collectives  56 us (22%)
  starting transfers between devices  34.1 us (13%)
  local copies, waits for them, and re-layouts  29 us (11%)
  between operations  13.6 us (5%)
  matrix products  8.63 us (3%)
    all_to_all x2, waiting for transfers between devices, copy_for_each(): return lax.all_to_all(copies, axis, split_axis=0, concat_axis=0, tiled=True)  52.8 us
    all_to_all x2, blocking collectives, copy_for_each(): return lax.all_to_all(copies, axis, split_axis=0, concat_axis=0, tiled=True)  41.3 us
    all_gather x1, waiting for transfers between devices, per_device(): con_cols = lax.all_gather(con_part, 'rowpt', axis=0, tiled=True)  37.6 us
    all_to_all x1, starting transfers between devices, per_device(): lax.all_to_all(orb_val, 'rowpt', split_axis=1, concat_axis=0, tiled=True)  17.3 us
    all_to_all x1, blocking collectives, sent_and_summed(): lax.all_to_all(in_blocks(array, dim, devices), axis, 0, 0, tiled=True)  14.8 us
    all_to_all x1, waiting for transfers between devices, per_device(): lax.all_to_all(orb_val, 'rowpt', split_axis=1, concat_axis=0, tiled=True)  14.1 us
    all_to_all x2, starting transfers between devices, copy_for_each(): return lax.all_to_all(copies, axis, split_axis=0, concat_axis=0, tiled=True)  8.85 us
    all_to_all x1, starting transfers between devices, per_device(): lax.all_to_all(orb_con, 'colpt', split_axis=1, concat_axis=0, tiled=True)  7.92 us
  transfers between devices with their start and end apart: 5, of which 5 were waited for; matrix products, arithmetic and copies ran while one was open for 6% of the time, Pallas kernels for 0%

commit v1 on v0

--- a/solution.py
+++ b/solution.py
@@ -51,7 +51,9 @@
     val_mixed = gathered_copies(val_part, "colpt", 0)
     val_cols = reorder_points(val_mixed, ncol, nrow)
     con_part = lax.all_to_all(orb_con, "colpt", split_axis=1, concat_axis=0, tiled=True)
-    con_cols = lax.all_gather(con_part, "rowpt", axis=0, tiled=True)
+    con_cols = jnp.concatenate(
+        lax.all_to_all(jnp.stack([con_part] * lax.axis_size("rowpt")), "rowpt", 0, 0), axis=0
+    )
     block_pts = min(NP, 2048)
     nblocks = NP // block_pts
     vecs = x_pairs.shape[0]

time: 253 us -> 289 us (1.14)
  waiting for transfers between devices: 108 us -> 149 us
  between operations: 13.6 us -> 0.2 us
  local copies, waits for them, and re-layouts: 29 us -> 36.9 us
  starting transfers between devices: 34.1 us -> 39.9 us
  blocking collectives: 56 us -> 51 us
    all_to_all x0 -> x1, waiting for transfers between devices: none -> 88.1 us  [per_device(): lax.all_to_all(jnp.stack([con_part] * lax.axis_size('rowpt')), 'rowpt', 0...]
    all_gather x1 -> x0, waiting for transfers between devices: 37.6 us -> none  [per_device(): con_cols = lax.all_gather(con_part, 'rowpt', axis=0, tiled=True)]
    all_to_all x2, waiting for transfers between devices: 52.8 us -> 42.5 us  [copy_for_each(): return lax.all_to_all(copies, axis, split_axis=0, concat_axis=0, tiled=True)]
    all_to_all x0 -> x1, starting transfers between devices: none -> 6.08 us  [per_device(): lax.all_to_all(jnp.stack([con_part] * lax.axis_size('rowpt')), 'rowpt', 0...]
    another operation x0 -> x3, local copies, waits for them, and re-layouts: none -> 5.03 us  [the longest x1 3.16 us: per_device(): con_blocks = con_cols.reshape(nblocks, block_pts, con_cols.shape[1])]
    all_to_all x1, blocking collectives: 14.8 us -> 10.5 us  [sent_and_summed(): lax.all_to_all(in_blocks(array, dim, devices), axis, 0, 0, tiled=True)]
    unnamed x13 -> x15, local copies, waits for them, and re-layouts: 6.1 us -> 5.37 us
  transfers between devices with their start and end apart: 5 -> 5, of which waited for: 5 -> 5; matrix products, arithmetic and copies ran while one was open for 6% -> 5% of each run, Pallas kernels for 0% -> 0%
where the time goes in v1:
time: 289 us; the launch traced here: 288 us
  waiting for transfers between devices  149 us (52%)
  blocking collectives  51 us (18%)
  starting transfers between devices  39.9 us (14%)
  local copies, waits for them, and re-layouts  36.9 us (13%)
  matrix products  8.63 us (3%)
    all_to_all x1, waiting for transfers between devices, per_device(): lax.all_to_all(jnp.stack([con_part] * lax.axis_size('rowpt')), 'rowpt', 0...  88.1 us
    all_to_all x2, waiting for transfers between devices, copy_for_each(): return lax.all_to_all(copies, axis, split_axis=0, concat_axis=0, tiled=True)  42.5 us
    all_to_all x2, blocking collectives, copy_for_each(): return lax.all_to_all(copies, axis, split_axis=0, concat_axis=0, tiled=True)  40.5 us
    all_to_all x1, starting transfers between devices, per_device(): lax.all_to_all(orb_val, 'rowpt', split_axis=1, concat_axis=0, tiled=True)  17.7 us
    all_to_all x1, waiting for transfers between devices, per_device(): lax.all_to_all(orb_val, 'rowpt', split_axis=1, concat_axis=0, tiled=True)  14.3 us
    all_to_all x2, starting transfers between devices, copy_for_each(): return lax.all_to_all(copies, axis, split_axis=0, concat_axis=0, tiled=True)  10.5 us
    all_to_all x1, blocking collectives, sent_and_summed(): lax.all_to_all(in_blocks(array, dim, devices), axis, 0, 0, tiled=True)  10.5 us
    all_to_all x1, starting transfers between devices, per_device(): lax.all_to_all(jnp.stack([con_part] * lax.axis_size('rowpt')), 'rowpt', 0...  6.08 us
  transfers between devices with their start and end apart: 5, of which 5 were waited for; matrix products, arithmetic and copies ran while one was open for 5% of the time, Pallas kernels for 0%

profile of v1, /device:TPU:33, one launch (start us, length us, event | category | flops | bytes accessed | tf_op | source)
XLA Modules:
  0.0 288.4 jit_solution(17308413831673159120)
XLA Ops:
  0.0 1.0 all_to_all.44
  2.0 17.7 %all-to-all-start = ((f32[32,1,512]{2,1,0:T(1,128)}), f32[32,1,512]{2,1,0:T(1,128)S(1)}, u32[]{:S(2)}, u32[]{:S(2)}) async-start(f32[32,1,512]{2,1,0:T(1,128)} %reshape.45), calls=%async_computation | async-start | bytes 131072 | tf_op jit(solution)/shard_map/all_to_all | solution.py:50
  21.4 14.3 %all-to-all-done = f32[32,1,512]{2,1,0:T(1,128)S(1)} async-done(((f32[32,1,512]{2,1,0:T(1,128)}), f32[32,1,512]{2,1,0:T(1,128)S(1)}, u32[]{:S(2)}, u32[]{:S(2)}) %all-to-all-start) | async-done | bytes 65568 | tf_op jit(solution)/shard_map/all_to_all | solution.py:50
  35.7 5.6 %all-to-all-start.2 = ((f32[16,1,1024]{2,1,0:T(1,128)}), f32[16,1,1024]{2,1,0:T(1,128)S(1)}, u32[]{:S(2)}, u32[]{:S(2)}) async-start(f32[16,1,1024]{2,1,0:T(1,128)} %reshape.47), calls=%async_computation.2 | async-start | bytes 131072 | tf_op jit(solution)/shard_map/all_to_all | solution.py:53
  43.0 4.1 %all-to-all-done.2 = f32[16,1,1024]{2,1,0:T(1,128)S(1)} async-done(((f32[16,1,1024]{2,1,0:T(1,128)}), f32[16,1,1024]{2,1,0:T(1,128)S(1)}, u32[]{:S(2)}, u32[]{:S(2)}) %all-to-all-start.2) | async-done | bytes 65568 | tf_op jit(solution)/shard_map/all_to_all | solution.py:53
  47.1 1.1 broadcast_in_dim.28
  48.2 5.2 %all-to-all-start.1 = ((f32[16,512,32]{1,2,0:T(8,128)}), f32[16,512,32]{1,2,0:T(8,128)S(1)}, u32[]{:S(2)}, u32[]{:S(2)}) async-start(f32[16,512,32]{1,2,0:T(8,128)} %broadcast_in_dim.28), calls=%async_computation.1 | async-start | bytes 2097152 | tf_op jit(solution)/shard_map/all_to_all | solution.py:17
  54.4 23.6 %all-to-all-done.1 = f32[16,512,32]{1,2,0:T(8,128)S(1)} async-done(((f32[16,512,32]{1,2,0:T(8,128)}), f32[16,512,32]{1,2,0:T(8,128)S(1)}, u32[]{:S(2)}, u32[]{:S(2)}) %all-to-all-start.1) | async-done | bytes 1048608 | tf_op jit(solution)/shard_map/all_to_all | solution.py:17
  78.0 1.8 stack.5
  79.8 6.1 %all-to-all-start.3 = ((f32[32,256,64]{1,2,0:T(8,128)}), f32[32,256,64]{1,2,0:T(8,128)S(1)}, u32[]{:S(2)}, u32[]{:S(2)}) async-start(f32[32,256,64]{1,2,0:T(8,128)} %stack.5), calls=%async_computation.3 | async-start | bytes 4194304 | tf_op jit(solution)/shard_map/all_to_all | solution.py:55
  85.9 3.6 %copy.52 = f32[16,512,32]{2,1,0:T(8,128)} copy(f32[16,512,32]{1,2,0:T(8,128)} %copy-done.1) | data formatting | bytes 2097152 | tf_op jit(solution)/shard_map/all_to_all | solution.py:17
  89.5 4.7 %copy.53 = f32[32,16,16,32]{3,2,1,0:T(8,128)} copy(f32[32,16,16,32]{3,2,0,1:T(8,128)} %bitcast.62) | data formatting | bytes 2097152 | tf_op jit(solution)/shard_map/transpose | solution.py:44
  94.2 3.6 %copy.63 = f32[4,2048,32]{1,2,0:T(8,128)} copy(f32[4,2048,32]{2,1,0:T(8,128)} %bitcast.63) | data formatting | bytes 2097152
  97.8 88.1 %all-to-all-done.3 = f32[32,256,64]{1,2,0:T(8,128)S(1)} async-done(((f32[32,256,64]{1,2,0:T(8,128)}), f32[32,256,64]{1,2,0:T(8,128)S(1)}, u32[]{:S(2)}, u32[]{:S(2)}) %all-to-all-start.3) | async-done | bytes 2097184 | tf_op jit(solution)/shard_map/all_to_all | solution.py:55
  185.9 2.6 copy.56
  188.5 3.2 %reshape_reshape.17 = f32[4,2048,64]{1,0,2:T(4,128)} reshape(f32[32,256,64]{1,0,2:T(8,128)} %copy.56) | data formatting | bytes 4194304 | tf_op jit(solution)/shard_map/reshape;reshape | solution.py:61
  191.7 2.8 copy.57
  194.5 8.2 %while.21 = (s32[]{:T(128)}, f32[4,4,2048]{2,1,0:T(4,128)S(1)}, f32[4,2048,64]{1,2,0:T(8,128)S(1)}, f32[4,32,64]{2,1,0:T(8,128)S(1)}, f32[4,2048,32]{1,2,0:T(8,128)}, /*index=5*/s32[]{:T(128)}) while((s32[]{:T(128)}, f32[4,4,2048]{2,1,0:T(4,128)S(1)}, f32[4,2048,64]{1,2,0:T(8,128)S(1)}, f32[4,32,64]{2,1,0:T(8,128)S(1)}, ...), condition=%wide.region_2.3_spmd, body=%wide.region_0.2_spmd.sunk | while | flops 201842688 | bytes 1474641 | solution.py:68
  195.5 1.0 fusion.21
  197.5 1.0 fusion.21
  199.6 1.0 fusion.21
  201.7 1.0 fusion.21
  203.0 10.5 %all_to_all.65 = f32[16,4,512]{2,1,0:T(4,128)S(1)} all-to-all(f32[16,4,512]{2,1,0:T(4,128)S(1)} %copy.60), channel_id=1, replica_groups=mesh['rowpt'=32,'colpt'=16] {'colpt'}, dimensions={0} | all-to-all | bytes 262144 | tf_op jit(solution)/shard_map/all_to_all | solution.py:32
  213.6 31.1 %all_to_all.66 = f32[32,4,512]{2,1,0:T(4,128)S(1)} all-to-all(f32[32,4,512]{2,1,0:T(4,128)S(1)} %broadcast_in_dim.30), channel_id=1, replica_groups=mesh['rowpt'=32,'colpt'=16] {'rowpt'}, dimensions={0} | all-to-all | bytes 524288 | tf_op jit(solution)/shard_map/all_to_all | solution.py:17
  245.3 9.4 %all_to_all.67 = f32[16,4,256]{2,1,0:T(4,128)S(1)} all-to-all(f32[16,4,256]{2,1,0:T(4,128)S(1)} %broadcast_in_dim.31), channel_id=1, replica_groups=mesh['rowpt'=32,'colpt'=16] {'colpt'}, dimensions={0} | all-to-all | bytes 131072 | tf_op jit(solution)/shard_map/all_to_all | solution.py:17
  255.4 5.3 %all-to-all-start.7 = ((f32[32,4,256]{2,1,0:T(4,128)}), f32[32,4,256]{2,1,0:T(4,128)S(1)}, u32[]{:S(2)}, u32[]{:S(2)}) async-start(f32[32,4,256]{2,1,0:T(4,128)} %broadcast_in_dim.32), calls=%async_computation.7 | async-start | bytes 262144 | tf_op jit(solution)/shard_map/all_to_all | solution.py:17
  260.8 19.0 %all-to-all-done.7 = f32[32,4,256]{2,1,0:T(4,128)S(1)} async-done(((f32[32,4,256]{2,1,0:T(4,128)}), f32[32,4,256]{2,1,0:T(4,128)S(1)}, u32[]{:S(2)}, u32[]{:S(2)}) %all-to-all-start.7) | async-done | bytes 131104 | tf_op jit(solution)/shard_map/all_to_all | solution.py:17
  279.7 8.0 %while.22 = (s32[]{:T(128)}, f32[4,32,64]{2,1,0:T(8,128)S(1)}, f32[4,2048,32]{1,2,0:T(8,128)}, f32[4,4,2048]{2,1,0:T(4,128)S(1)}, f32[4,2048,64]{1,2,0:T(8,128)S(1)}, /*index=5*/s32[]{:T(128)}, s32[]{:T(128)}) while((s32[]{:T(128)}, f32[4,32,64]{2,1,0:T(8,128)S(1)}, f32[4,2048,32]{1,2,0:T(8,128)}, f32[4,4,2048]{2,1,0:T(4,128)S(1)}, ...), condition=%wide.region_7.8_spmd.clone, body=%wide.region_6.7_spmd.clone.sunk | while | flops 201605120 | bytes 1507427 | solution.py:84
  280.7 1.0 convolution_add_fusion.2
  282.7 1.0 convolution_add_fusion.2
  284.8 1.0 convolution_add_fusion.2
  286.8 1.0 convolution_add_fusion.2
  (52 shorter events, 15.5 us)
Async XLA Ops:
  0.0 244.8 %copy-start = (f32[256,512]{1,0:T(8,128)S(1)}, f32[256,512]{1,0:T(8,128)}, u32[]{:S(2)}) copy-start(f32[256,512]{1,0:T(8,128)} %param.15) | copy-start | bytes 1572868
  2.0 33.7 %all-to-all-start = ((f32[32,1,512]{2,1,0:T(1,128)}), f32[32,1,512]{2,1,0:T(1,128)S(1)}, u32[]{:S(2)}, u32[]{:S(2)}) async-start(f32[32,1,512]{2,1,0:T(1,128)} %reshape.45), calls=%async_computation | async-start | bytes 131072 | tf_op jit(solution)/shard_map/all_to_all | solution.py:50
  35.7 11.4 %all-to-all-start.2 = ((f32[16,1,1024]{2,1,0:T(1,128)}), f32[16,1,1024]{2,1,0:T(1,128)S(1)}, u32[]{:S(2)}, u32[]{:S(2)}) async-start(f32[16,1,1024]{2,1,0:T(1,128)} %reshape.47), calls=%async_computation.2 | async-start | bytes 131072 | tf_op jit(solution)/shard_map/all_to_all | solution.py:53
  48.2 29.8 %all-to-all-start.1 = ((f32[16,512,32]{1,2,0:T(8,128)}), f32[16,512,32]{1,2,0:T(8,128)S(1)}, u32[]{:S(2)}, u32[]{:S(2)}) async-start(f32[16,512,32]{1,2,0:T(8,128)} %broadcast_in_dim.28), calls=%async_computation.1 | async-start | bytes 2097152 | tf_op jit(solution)/shard_map/all_to_all | solution.py:17
  78.0 1.8 copy-start.1
  79.8 106.1 %all-to-all-start.3 = ((f32[32,256,64]{1,2,0:T(8,128)}), f32[32,256,64]{1,2,0:T(8,128)S(1)}, u32[]{:S(2)}, u32[]{:S(2)}) async-start(f32[32,256,64]{1,2,0:T(8,128)} %stack.5), calls=%async_computation.3 | async-start | bytes 4194304 | tf_op jit(solution)/shard_map/all_to_all | solution.py:55
  191.7 2.8 copy-start.2
  202.7 58.0 %copy-start.3 = (f32[32]{0:T(128)S(1)}, f32[32]{0:T(128)}, u32[]{:S(2)}) copy-start(f32[32]{0:T(128)} %param.11) | copy-start | bytes 388
  202.7 58.0 %copy-start.4 = (f32[64]{0:T(128)S(1)}, f32[64]{0:T(128)}, u32[]{:S(2)}) copy-start(f32[64]{0:T(128)} %param.12) | copy-start | bytes 772
  255.4 24.3 %all-to-all-start.7 = ((f32[32,4,256]{2,1,0:T(4,128)}), f32[32,4,256]{2,1,0:T(4,128)S(1)}, u32[]{:S(2)}, u32[]{:S(2)}) async-start(f32[32,4,256]{2,1,0:T(4,128)} %broadcast_in_dim.32), calls=%async_computation.7 | async-start | bytes 262144 | tf_op jit(solution)/shard_map/all_to_all | solution.py:17
